TPU v7x, 32 devices: a whole 2x2x4 slice. The times are simulated.
32 devices in a mesh: dp: 16 (over z, x, core), tile: 2 (over y).
Axes of the slice: x: 2, y: 2, z: 4, core: 2. Of those that a mesh axis runs over, the one named last changes fastest.
Arguments:
- proposal_boxes: int32 [16, 4, 512], P('dp'), may hold values from 0 to 672, as said below
- level_plan: int32 [16, 512], P('dp'), may hold values from 0 to 1
- fine_map: bfloat16 [16, 84, 168, 128], P('dp', 'tile'), may hold values from -6 to 6
- coarse_map: bfloat16 [16, 42, 84, 128], P('dp', 'tile'), may hold values from -6 to 6
- first_weight: bfloat16 [6272, 1024], P('tile', 'dp'), may hold values from -0.078125 to 0.078125
- second_weight: bfloat16 [1024, 1024], P('tile', 'dp'), may hold values from -0.1875 to 0.1875
- upstream: bfloat16 [16, 512, 1024], P('dp'), may hold values from -6 to 6
Outputs:
- first_grad: float32 [6272, 1024], P('tile', 'dp')
- second_grad: float32 [1024, 1024], P('tile', 'dp')
Inputs may be any that keep to these rules, and one draw needn't show every extreme that they name: `proposal_boxes`: with s = 4 where level_plan is 0 and s = 8 where it is 1: h >= 1, w >= 1, y0 + h <= 336, x0 + w <= 672, (y0 mod s) + h <= 14 * s and (x0 mod s) + w <= 14 * s. Band b holds the proposals with b * 168 <= y0 < (b + 1) * 168; at most 256 of an image's proposals lie in one band, and in every image some band holds exactly 256.
All inputs are finite; a program needn't handle non-finite values.
Results may differ from a plain program's by a relative error of at most 0.017.
Values may be sent and summed in bfloat16 or wider, within the bound.
A program may use at most 64 MiB of HBM per device.

v0:
```python
import jax
import jax.numpy as jnp
from jax import lax
from jax.sharding import PartitionSpec as P

WIN = 16


def from_behind(block, axis, distance):
    devices = range(lax.axis_size(axis))
    route = [(i - distance, i) for i in devices if i - distance in devices]
    return lax.ppermute(block, axis, route)


def gelu_parts(hidden):
    factor = 0.7978845608028654
    cubic_term = 0.044715
    inner_term = factor * (hidden + cubic_term * hidden * hidden * hidden)
    tangent = jnp.tanh(inner_term)
    gelu_value = 0.5 * hidden * (1.0 + tangent)
    gelu_slope = 0.5 * (1.0 + tangent) + 0.5 * hidden * (1.0 - tangent * tangent) * factor * (
        1.0 + 3.0 * cubic_term * hidden * hidden
    )
    return (gelu_value, gelu_slope)


def block_size():
    return 16


def sample_weights(begin_px, extent, stride, cell_pos):
    stride_float = stride.astype(jnp.float32)[:, None]
    bin_index = jnp.arange(7, dtype=jnp.float32)[None, :]
    sample_pos = begin_px.astype(jnp.float32)[:, None] / stride_float + (
        bin_index + 0.5
    ) * extent.astype(jnp.float32)[:, None] / (7.0 * stride_float)
    return jnp.maximum(0.0, 1.0 - jnp.abs(sample_pos[:, :, None] - cell_pos[None, None, :]))


def crop_block(combined, fields, levels_blk, live_slot, row_pos, fine_part, col_pos):
    top_pixel = fields[0]
    left_pixel = fields[1]
    height = fields[2]
    box_width = fields[3]
    stride = jnp.where(levels_blk == 0, 4, 8).astype(jnp.int32)
    level_match = (fine_part[None, :] == (levels_blk == 0)[:, None]).astype(jnp.float32)
    row_mask = level_match * live_slot.astype(jnp.float32)[:, None]
    row_low = (sample_weights(top_pixel, height, stride, row_pos) * row_mask[:, None, :]).astype(
        jnp.bfloat16
    )
    col_low = sample_weights(left_pixel, box_width, stride, col_pos).astype(jnp.bfloat16)
    count = levels_blk.shape[0]
    total_rows, total_cols, channels = combined.shape
    by_column = lax.dot_general(
        col_low.reshape(count * 7, total_cols),
        combined,
        (((1,), (1,)), ((), ())),
        preferred_element_type=jnp.float32,
    )
    by_column = by_column.reshape(count, 7, total_rows, channels)
    crop_rows = jnp.einsum(
        "bia,bjac->bijc", row_low.astype(jnp.float32), by_column, precision=lax.Precision.HIGHEST
    )
    return crop_rows.reshape(count, 49 * channels).astype(jnp.bfloat16)


def per_device(
    proposal_boxes, level_plan, fine_map, coarse_map, first_weight, second_weight, upstream
):
    tile_count = lax.axis_size("tile")
    band_index = lax.axis_index("tile")
    num_props = level_plan.shape[1]
    capacity = max(num_props // 4, num_props // tile_count)
    fine_tile = fine_map[0]
    coarse = coarse_map[0]
    fine_rows, fine_cols, channels = fine_tile.shape
    coarse_rows, coarse_cols = (coarse.shape[0], coarse.shape[1])
    fields = proposal_boxes[0]
    levels_img = level_plan[0]
    owner_band = fields[0] // (4 * fine_rows)
    members = (owner_band[:, None] == jnp.arange(tile_count, dtype=jnp.int32)[None, :]).astype(
        jnp.int32
    )
    slot_rank = jnp.sum((jnp.cumsum(members, axis=0) - 1) * members, axis=1)
    slot_id = owner_band * capacity + slot_rank
    target = jnp.where(owner_band == band_index, slot_rank, capacity)
    slot_prop = (
        jnp.full((capacity,), num_props, jnp.int32)
        .at[target]
        .set(jnp.arange(num_props, dtype=jnp.int32), mode="drop")
    )
    live_slot = (slot_prop < num_props).astype(jnp.int32)
    chosen = jnp.minimum(slot_prop, num_props - 1)
    slot_fields = jnp.take(fields, chosen, axis=1)
    slot_levels = jnp.take(levels_img, chosen)
    top_rows = jnp.concatenate([fine_tile[:WIN], coarse[:WIN]], axis=1)
    below_rows = from_behind(top_rows, "tile", -1)
    fine_ext = jnp.concatenate([fine_tile, below_rows[:, :fine_cols]], axis=0)
    coarse_ext = jnp.concatenate([coarse, below_rows[:, fine_cols:]], axis=0)
    coarse_ext = jnp.pad(coarse_ext, ((0, 0), (0, fine_cols - coarse_cols), (0, 0)))
    combined = jnp.concatenate([fine_ext, coarse_ext], axis=0)
    fine_count = fine_rows + WIN
    coarse_count = coarse_rows + WIN
    fine_pos = (band_index * fine_rows).astype(jnp.float32) + jnp.arange(
        fine_count, dtype=jnp.float32
    )
    coarse_pos = (band_index * coarse_rows).astype(jnp.float32) + jnp.arange(
        coarse_count, dtype=jnp.float32
    )
    row_pos = jnp.concatenate([fine_pos, coarse_pos], axis=0)
    fine_part = jnp.arange(fine_count + coarse_count) < fine_count
    col_pos = jnp.arange(fine_cols, dtype=jnp.float32)
    block_len = block_size()
    grouped_fields = slot_fields.reshape(4, capacity // block_len, block_len).transpose(1, 0, 2)
    grouped_levels = slot_levels.reshape(capacity // block_len, block_len)
    grouped_live = live_slot.reshape(capacity // block_len, block_len)

    def crop_group(pieces):
        part_fields, part_levels, part_live = pieces
        return crop_block(
            combined, part_fields, part_levels, part_live, row_pos, fine_part, col_pos
        )

    crop_rows = lax.map(crop_group, (grouped_fields, grouped_levels, grouped_live)).reshape(
        capacity, 49 * channels
    )
    received = lax.all_to_all(crop_rows, "tile", split_axis=1, concat_axis=0, tiled=True)
    own_feats = jnp.take(received, slot_id, axis=0)
    partial_hidden = jnp.dot(
        own_feats,
        lax.all_gather(first_weight, "dp", axis=1, tiled=True),
        preferred_element_type=jnp.float32,
    )
    share_width = partial_hidden.shape[1] // tile_count
    upstream_rows = upstream[0]
    second_rows = lax.all_gather(second_weight, "dp", axis=1, tiled=True)
    pieces = lax.all_to_all(
        partial_hidden.astype(jnp.bfloat16), "tile", split_axis=1, concat_axis=0, tiled=True
    ).astype(partial_hidden.dtype)
    hidden_own = jnp.sum(pieces.reshape(tile_count, num_props, share_width), axis=0)
    gelu_value, gelu_slope = gelu_parts(hidden_own)
    activated = gelu_value.astype(jnp.bfloat16)
    back_grad = lax.dot_general(
        upstream_rows, second_rows, (((1,), (1,)), ((), ())), preferred_element_type=jnp.float32
    )
    pre_own = (back_grad * gelu_slope).astype(jnp.bfloat16)
    pre_grad = lax.all_gather(pre_own, "tile", axis=1, tiled=True)
    second_grad = lax.psum_scatter(
        lax.dot_general(
            upstream_rows, activated, (((0,), (0,)), ((), ())), preferred_element_type=jnp.float32
        ),
        "dp",
        scatter_dimension=0,
        tiled=True,
    ).T
    first_grad = lax.psum_scatter(
        lax.dot_general(
            pre_grad, own_feats, (((0,), (0,)), ((), ())), preferred_element_type=jnp.float32
        ),
        "dp",
        scatter_dimension=0,
        tiled=True,
    ).T
    return (first_grad, second_grad)


def solution(mesh):
    placed = (
        P("dp", None, None),
        P("dp", None),
        P("dp", "tile", None, None),
        P("dp", "tile", None, None),
        P("tile", "dp"),
        P("tile", "dp"),
        P("dp", None, None),
    )
    return jax.shard_map(
        per_device,
        mesh=mesh,
        in_specs=placed,
        out_specs=(P("tile", "dp"), P("tile", "dp")),
        check_vma=False,
    )
```

profile of v0, /device:TPU:0, one launch (start us, length us, event | category | flops | bytes accessed | tf_op | source)
XLA Modules:
  0.0 588.8 jit_solution(6103407495157874907)
XLA Ops:
  18.4 18.8 %collective-permute-done = bf16[16,252,128]{2,0,1:T(8,128)(2,1)S(1)} collective-permute-done((bf16[16,252,128]{2,0,1:T(8,128)(2,1)}, bf16[16,252,128]{2,0,1:T(8,128)(2,1)S(1)}, u32[]{:S(2)}, u32[]{:S(2)}) %collective-permute-start) | collective-permute-done | bytes 1032224 | tf_op jit(solution)/shard_map/ppermute | solution.py:12
  41.5 209.6 %while.11 = (s32[]{:T(128)}, bf16[16,16,6272]{2,1,0:T(8,128)(2,1)}, s32[16,4,16]{2,1,0:T(4,128)S(1)}, s32[16,16]{1,0:T(8,128)S(1)}, f32[95]{0:T(128)S(1)}, /*ind...) while((s32[]{:T(128)}, bf16[16,16,6272]{2,1,0:T(8,128)(2,1)}, ...), condition=%wide.region_5.6_spmd.clone, body=%wide.region_4.5_spmd.clone.sunk | while | flops 572268672 | bytes 16403843 | solution.py:124
  47.3 6.3 %fusion.76 = bf16[16,7,7,128]{3,1,2,0:T(8,128)(2,1)S(1)} fusion(f32[16,7,95,128]{3,0,2,1:T(8,128)} %fusion.74, f32[16,95]{1,0:T(8,128)S(1)} %compare_select_fusion.8, f32[95]{0:T(128)S(1)} %get-tuple-element.182, f32[16,7]{1,0:T(8,128)S(1)} %copy.68), kind=kOutput, calls=%fused_computation.10.clone.1 | convolution fusion | flops 114565472 | bytes 5655292 | tf_op jit(solution)/shard_map/while/body/eval_jaxpr/bia,bjac->bijc/dot_general | solution.py:61
  60.4 6.4 %fusion.76 = bf16[16,7,7,128]{3,1,2,0:T(8,128)(2,1)S(1)} fusion(f32[16,7,95,128]{3,0,2,1:T(8,128)} %fusion.74, f32[16,95]{1,0:T(8,128)S(1)} %compare_select_fusion.8, f32[95]{0:T(128)S(1)} %get-tuple-element.182, f32[16,7]{1,0:T(8,128)S(1)} %copy.68), kind=kOutput, calls=%fused_computation.10.clone.1 | convolution fusion | flops 114565472 | bytes 5655292 | tf_op jit(solution)/shard_map/while/body/eval_jaxpr/bia,bjac->bijc/dot_general | solution.py:61
  73.5 6.4 %fusion.76 = bf16[16,7,7,128]{3,1,2,0:T(8,128)(2,1)S(1)} fusion(f32[16,7,95,128]{3,0,2,1:T(8,128)} %fusion.74, f32[16,95]{1,0:T(8,128)S(1)} %compare_select_fusion.8, f32[95]{0:T(128)S(1)} %get-tuple-element.182, f32[16,7]{1,0:T(8,128)S(1)} %copy.68), kind=kOutput, calls=%fused_computation.10.clone.1 | convolution fusion | flops 114565472 | bytes 5655292 | tf_op jit(solution)/shard_map/while/body/eval_jaxpr/bia,bjac->bijc/dot_general | solution.py:61
  81.1 5.5 fusion.74
  86.7 6.3 %fusion.76 = bf16[16,7,7,128]{3,1,2,0:T(8,128)(2,1)S(1)} fusion(f32[16,7,95,128]{3,0,2,1:T(8,128)} %fusion.74, f32[16,95]{1,0:T(8,128)S(1)} %compare_select_fusion.8, f32[95]{0:T(128)S(1)} %get-tuple-element.182, f32[16,7]{1,0:T(8,128)S(1)} %copy.68), kind=kOutput, calls=%fused_computation.10.clone.1 | convolution fusion | flops 114565472 | bytes 5655292 | tf_op jit(solution)/shard_map/while/body/eval_jaxpr/bia,bjac->bijc/dot_general | solution.py:61
  99.8 6.3 %fusion.76 = bf16[16,7,7,128]{3,1,2,0:T(8,128)(2,1)S(1)} fusion(f32[16,7,95,128]{3,0,2,1:T(8,128)} %fusion.74, f32[16,95]{1,0:T(8,128)S(1)} %compare_select_fusion.8, f32[95]{0:T(128)S(1)} %get-tuple-element.182, f32[16,7]{1,0:T(8,128)S(1)} %copy.68), kind=kOutput, calls=%fused_computation.10.clone.1 | convolution fusion | flops 114565472 | bytes 5655292 | tf_op jit(solution)/shard_map/while/body/eval_jaxpr/bia,bjac->bijc/dot_general | solution.py:61
  107.2 5.5 fusion.74
  112.9 6.3 %fusion.76 = bf16[16,7,7,128]{3,1,2,0:T(8,128)(2,1)S(1)} fusion(f32[16,7,95,128]{3,0,2,1:T(8,128)} %fusion.74, f32[16,95]{1,0:T(8,128)S(1)} %compare_select_fusion.8, f32[95]{0:T(128)S(1)} %get-tuple-element.182, f32[16,7]{1,0:T(8,128)S(1)} %copy.68), kind=kOutput, calls=%fused_computation.10.clone.1 | convolution fusion | flops 114565472 | bytes 5655292 | tf_op jit(solution)/shard_map/while/body/eval_jaxpr/bia,bjac->bijc/dot_general | solution.py:61
  120.3 5.5 fusion.74
  126.0 6.3 %fusion.76 = bf16[16,7,7,128]{3,1,2,0:T(8,128)(2,1)S(1)} fusion(f32[16,7,95,128]{3,0,2,1:T(8,128)} %fusion.74, f32[16,95]{1,0:T(8,128)S(1)} %compare_select_fusion.8, f32[95]{0:T(128)S(1)} %get-tuple-element.182, f32[16,7]{1,0:T(8,128)S(1)} %copy.68), kind=kOutput, calls=%fused_computation.10.clone.1 | convolution fusion | flops 114565472 | bytes 5655292 | tf_op jit(solution)/shard_map/while/body/eval_jaxpr/bia,bjac->bijc/dot_general | solution.py:61
  139.1 6.3 %fusion.76 = bf16[16,7,7,128]{3,1,2,0:T(8,128)(2,1)S(1)} fusion(f32[16,7,95,128]{3,0,2,1:T(8,128)} %fusion.74, f32[16,95]{1,0:T(8,128)S(1)} %compare_select_fusion.8, f32[95]{0:T(128)S(1)} %get-tuple-element.182, f32[16,7]{1,0:T(8,128)S(1)} %copy.68), kind=kOutput, calls=%fused_computation.10.clone.1 | convolution fusion | flops 114565472 | bytes 5655292 | tf_op jit(solution)/shard_map/while/body/eval_jaxpr/bia,bjac->bijc/dot_general | solution.py:61
  152.2 6.3 %fusion.76 = bf16[16,7,7,128]{3,1,2,0:T(8,128)(2,1)S(1)} fusion(f32[16,7,95,128]{3,0,2,1:T(8,128)} %fusion.74, f32[16,95]{1,0:T(8,128)S(1)} %compare_select_fusion.8, f32[95]{0:T(128)S(1)} %get-tuple-element.182, f32[16,7]{1,0:T(8,128)S(1)} %copy.68), kind=kOutput, calls=%fused_computation.10.clone.1 | convolution fusion | flops 114565472 | bytes 5655292 | tf_op jit(solution)/shard_map/while/body/eval_jaxpr/bia,bjac->bijc/dot_general | solution.py:61
  165.3 6.3 %fusion.76 = bf16[16,7,7,128]{3,1,2,0:T(8,128)(2,1)S(1)} fusion(f32[16,7,95,128]{3,0,2,1:T(8,128)} %fusion.74, f32[16,95]{1,0:T(8,128)S(1)} %compare_select_fusion.8, f32[95]{0:T(128)S(1)} %get-tuple-element.182, f32[16,7]{1,0:T(8,128)S(1)} %copy.68), kind=kOutput, calls=%fused_computation.10.clone.1 | convolution fusion | flops 114565472 | bytes 5655292 | tf_op jit(solution)/shard_map/while/body/eval_jaxpr/bia,bjac->bijc/dot_general | solution.py:61
  178.4 6.3 %fusion.76 = bf16[16,7,7,128]{3,1,2,0:T(8,128)(2,1)S(1)} fusion(f32[16,7,95,128]{3,0,2,1:T(8,128)} %fusion.74, f32[16,95]{1,0:T(8,128)S(1)} %compare_select_fusion.8, f32[95]{0:T(128)S(1)} %get-tuple-element.182, f32[16,7]{1,0:T(8,128)S(1)} %copy.68), kind=kOutput, calls=%fused_computation.10.clone.1 | convolution fusion | flops 114565472 | bytes 5655292 | tf_op jit(solution)/shard_map/while/body/eval_jaxpr/bia,bjac->bijc/dot_general | solution.py:61
  191.4 6.3 %fusion.76 = bf16[16,7,7,128]{3,1,2,0:T(8,128)(2,1)S(1)} fusion(f32[16,7,95,128]{3,0,2,1:T(8,128)} %fusion.74, f32[16,95]{1,0:T(8,128)S(1)} %compare_select_fusion.8, f32[95]{0:T(128)S(1)} %get-tuple-element.182, f32[16,7]{1,0:T(8,128)S(1)} %copy.68), kind=kOutput, calls=%fused_computation.10.clone.1 | convolution fusion | flops 114565472 | bytes 5655292 | tf_op jit(solution)/shard_map/while/body/eval_jaxpr/bia,bjac->bijc/dot_general | solution.py:61
  204.5 6.3 %fusion.76 = bf16[16,7,7,128]{3,1,2,0:T(8,128)(2,1)S(1)} fusion(f32[16,7,95,128]{3,0,2,1:T(8,128)} %fusion.74, f32[16,95]{1,0:T(8,128)S(1)} %compare_select_fusion.8, f32[95]{0:T(128)S(1)} %get-tuple-element.182, f32[16,7]{1,0:T(8,128)S(1)} %copy.68), kind=kOutput, calls=%fused_computation.10.clone.1 | convolution fusion | flops 114565472 | bytes 5655292 | tf_op jit(solution)/shard_map/while/body/eval_jaxpr/bia,bjac->bijc/dot_general | solution.py:61
  217.6 6.3 %fusion.76 = bf16[16,7,7,128]{3,1,2,0:T(8,128)(2,1)S(1)} fusion(f32[16,7,95,128]{3,0,2,1:T(8,128)} %fusion.74, f32[16,95]{1,0:T(8,128)S(1)} %compare_select_fusion.8, f32[95]{0:T(128)S(1)} %get-tuple-element.182, f32[16,7]{1,0:T(8,128)S(1)} %copy.68), kind=kOutput, calls=%fused_computation.10.clone.1 | convolution fusion | flops 114565472 | bytes 5655292 | tf_op jit(solution)/shard_map/while/body/eval_jaxpr/bia,bjac->bijc/dot_general | solution.py:61
  230.7 6.3 %fusion.76 = bf16[16,7,7,128]{3,1,2,0:T(8,128)(2,1)S(1)} fusion(f32[16,7,95,128]{3,0,2,1:T(8,128)} %fusion.74, f32[16,95]{1,0:T(8,128)S(1)} %compare_select_fusion.8, f32[95]{0:T(128)S(1)} %get-tuple-element.182, f32[16,7]{1,0:T(8,128)S(1)} %copy.68), kind=kOutput, calls=%fused_computation.10.clone.1 | convolution fusion | flops 114565472 | bytes 5655292 | tf_op jit(solution)/shard_map/while/body/eval_jaxpr/bia,bjac->bijc/dot_general | solution.py:61
  243.8 6.3 %fusion.76 = bf16[16,7,7,128]{3,1,2,0:T(8,128)(2,1)S(1)} fusion(f32[16,7,95,128]{3,0,2,1:T(8,128)} %fusion.74, f32[16,95]{1,0:T(8,128)S(1)} %compare_select_fusion.8, f32[95]{0:T(128)S(1)} %get-tuple-element.182, f32[16,7]{1,0:T(8,128)S(1)} %copy.68), kind=kOutput, calls=%fused_computation.10.clone.1 | convolution fusion | flops 114565472 | bytes 5655292 | tf_op jit(solution)/shard_map/while/body/eval_jaxpr/bia,bjac->bijc/dot_general | solution.py:61
  251.1 8.0 %all_to_all.24 = bf16[256,2,3136]{2,1,0:T(2,128)(2,1)} reshape(bf16[16,16,6272]{2,1,0:T(8,128)(2,1)} %get-tuple-element.49) | data formatting | bytes 6422528 | tf_op jit(solution)/shard_map/all_to_all | solution.py:127
  259.0 9.1 %copy.40 = bf16[256,2,3136]{0,2,1:T(8,128)(2,1)} copy(bf16[256,2,3136]{2,1,0:T(2,128)(2,1)} %all_to_all.24) | data formatting | bytes 6422528 | tf_op jit(solution)/shard_map/all_to_all | solution.py:127
  274.4 35.9 %all-to-all-done = bf16[256,2,3136]{0,2,1:T(8,128)(2,1)} async-done(((bf16[256,2,3136]{0,2,1:T(8,128)(2,1)}), bf16[256,2,3136]{0,2,1:T(8,128)(2,1)}, u32[]{:S(2)}, u32[]{:S(2)}) %all-to-all-start) | async-done | bytes 3211296 | tf_op jit(solution)/shard_map/all_to_all | solution.py:127
  310.3 5.7 copy.41
  315.9 9.6 %gather_fusion.2 = bf16[512,3136]{1,0:T(8,128)(2,1)} fusion(bf16[512,3136]{1,0:T(8,128)(2,1)} %bitcast.104, s32[1024]{0:T(1024)S(1)} %pad_clamp_fusion), kind=kCustom, calls=%fused_computation.2 | custom fusion | bytes 6424576 | tf_op jit(solution)/shard_map/jit(_take)/gather | solution.py:128
  325.5 7.6 %convolution_convert_fusion = bf16[512,1024]{1,0:T(8,128)(2,1)S(1)} fusion(bf16[3136,1024]{0,1:T(8,128)(2,1)} %all-gather.6.cloned.1.call-done, bf16[512,3136]{1,0:T(8,128)(2,1)} %gather_fusion.2, pred[512]{0:T(512)(128)(4,1)S(1)} %compare_and_fusion.2), kind=kOutput, calls=%fused_computation.59 | convolution fusion | flops 3290464256 | bytes 10682880 | tf_op jit(solution)/shard_map/dot_general | solution.py:129
  333.2 15.2 %all_to_all.32 = bf16[512,2,512]{2,0,1:T(8,128)(2,1)S(1)} all-to-all(bf16[512,2,512]{2,0,1:T(8,128)(2,1)S(1)} %bitcast.105), channel_id=1, replica_groups=mesh['dp'=16,'tile'=2] {'tile'}, dimensions={1} | all-to-all | bytes 2097152 | tf_op jit(solution)/shard_map/all_to_all | solution.py:137
  356.5 17.7 %all-gather.8.cloned.1.call-done = bf16[512,1024]{1,0:T(8,128)(2,1)} async-done(((bf16[512,512]{1,0:T(8,128)(2,1)}), bf16[512,1024]{1,0:T(8,128)(2,1)}) %all-gather.8.cloned.1.call-update) | async-done | bytes 1048592 | tf_op jit(solution)/shard_map/all_gather | solution.py:147
  374.2 10.8 %fusion.36 = f32[1024,3136]{1,0:T(8,128)} fusion(bf16[512,1024]{1,0:T(8,128)(2,1)} %all-gather.8.cloned.1.call-done, bf16[512,3136]{1,0:T(8,128)(2,1)} %gather_fusion.2, pred[512]{0:T(512)(128)(4,1)S(1)} %compare_and_fusion.2), kind=kOutput, calls=%fused_computation.61 | convolution fusion | flops 3289939968 | bytes 17105408 | tf_op jit(solution)/shard_map/dot_general | solution.py:157
  385.0 55.2 %reduce-scatter.7.cloned.1.call-done = f32[64,512]{1,0:T(8,128)} async-done(((f32[1024,512]{1,0:T(8,128)}), f32[64,512]{1,0:T(8,128)}) %reduce-scatter.7.cloned.1.call-update) | async-done | bytes 131088
  440.2 142.1 %reduce-scatter.5.cloned.1.call-done = f32[64,3136]{1,0:T(8,128)} async-done(((f32[1024,3136]{1,0:T(8,128)}), f32[64,3136]{1,0:T(8,128)}) %reduce-scatter.5.cloned.1.call-update) | async-done | bytes 802832 | tf_op jit(solution)/shard_map/reduce_scatter | solution.py:156
  (295 shorter events, 121.2 us)
Async XLA Ops:
  7.2 341.5 %copy-start = (bf16[1,512,1024]{2,1,0:T(8,128)(2,1)S(1)}, bf16[1,512,1024]{2,1,0:T(8,128)(2,1)}, u32[]{:S(2)}) copy-start(bf16[1,512,1024]{2,1,0:T(8,128)(2,1)} %param.15) | copy-start | bytes 3145732
  7.2 1.5 slice-start
  7.2 4.1 copy-start.5
  7.2 318.3 %all-gather.6.cloned.1.call-start = ((), (), s32[]{:S(2)}) async-start(), calls=%async_computation.5 | async-start | bytes 6963200 | tf_op jit(solution)/shard_map/all_gather | solution.py:131
  8.5 7.6 %copy-start.1 = (s32[1,512]{1,0:T(1,128)S(1)}, s32[1,512]{1,0:T(1,128)}, u32[]{:S(2)}) copy-start(s32[1,512]{1,0:T(1,128)} %param.10) | copy-start | bytes 6148
  9.8 27.9 %copy-start.3 = (bf16[1,21,84,128]{3,2,1,0:T(8,128)(2,1)S(1)}, bf16[1,21,84,128]{3,2,1,0:T(8,128)(2,1)}, u32[]{:S(2)}) copy-start(bf16[1,21,84,128]{3,2,1,0:T(8,128)(2,1)} %param.12) | copy-start | bytes 1354756
  9.8 27.4 %collective-permute-start = (bf16[16,252,128]{2,0,1:T(8,128)(2,1)}, bf16[16,252,128]{2,0,1:T(8,128)(2,1)S(1)}, u32[]{:S(2)}, u32[]{:S(2)}) collective-permute-start(bf16[16,252,128]{2,0,1:T(8,128)(2,1)} %pad_maximum_fusion.1), channel_id=1, source_target_pairs={{1,0},{3,2},{5,4},{7,6},{9,8},{11,10},{13,12},{15,14},{17,16},{19,... | collective-permute-start | bytes 3096584 | tf_op jit(solution)/shard_map/ppermute | solution.py:12
  18.4 19.5 %copy-start.2 = (bf16[1,42,168,128]{3,2,1,0:T(8,128)(2,1)S(1)}, bf16[1,42,168,128]{3,2,1,0:T(8,128)(2,1)}, u32[]{:S(2)}) copy-start(bf16[1,42,168,128]{3,2,1,0:T(8,128)(2,1)} %param.11) | copy-start | bytes 5419012
  268.1 42.1 %all-to-all-start = ((bf16[256,2,3136]{0,2,1:T(8,128)(2,1)}), bf16[256,2,3136]{0,2,1:T(8,128)(2,1)}, u32[]{:S(2)}, u32[]{:S(2)}) async-start(bf16[256,2,3136]{0,2,1:T(8,128)(2,1)} %copy.40), calls=%async_computation | async-start | bytes 6422528 | tf_op jit(solution)/shard_map/all_to_all | solution.py:127
  273.4 75.3 %all-gather.4.cloned.1.call-start = ((), (), s32[]{:S(2)}) async-start(), calls=%async_computation.4 | async-start | bytes 1114112 | tf_op jit(solution)/shard_map/all_gather | solution.py:136
  274.1 100.1 %all-gather.8.cloned.1.call-start = ((), (), s32[]{:S(2)}) async-start(), calls=%async_computation.6 | async-start | bytes 1572864 | tf_op jit(solution)/shard_map/all_gather | solution.py:147
  348.6 3.6 copy-start.4
  352.2 88.0 %reduce-scatter.7.cloned.1.call-start = ((), (), s32[]{:S(2)}) async-start(), calls=%async_computation.8 | async-start | bytes 2228224
  356.2 226.1 %reduce-scatter.5.cloned.1.call-start = ((), (), s32[]{:S(2)}) async-start(), calls=%async_computation.7 | async-start | bytes 13926400 | tf_op jit(solution)/shard_map/reduce_scatter | solution.py:156
Sparse Core Ops, SparseCore 0:
  11.4 66.7 all-gather.5
  276.4 40.3 all-gather.3
  352.3 21.8 all-gather.7
  378.4 61.7 reduce-scatter.6
  444.7 137.5 reduce-scatter.4
where the time goes:
time: 591 us; the launch traced here: 589 us
  waiting for transfers between devices  270 us (46%)
  matrix products  213 us (36%)
  local copies, waits for them, and re-layouts  59.2 us (10%)
  blocking collectives  15.2 us (3%)
  between operations  14.1 us (2%)
  other arithmetic  9.25 us (2%)
  starting transfers between devices  7.24 us (1%)
    reduce_scatter x1, waiting for transfers between devices, per_device(): lax.psum_scatter(lax.dot_general(pre_grad, own_feats, (((0,), (0,)), ((),...  142 us
    dot_general x16, matrix products, crop_block(): jnp.einsum('bia,bjac->bijc', row_low.astype(jnp.float32), by_column, prec...  101 us
    dot_general x16, matrix products, crop_block(): lax.dot_general(col_low.reshape(count * 7, total_cols), combined, (((1,),...  88.1 us
    unnamed x6, waiting for transfers between devices  55.9 us
    all_to_all x1, waiting for transfers between devices, per_device(): lax.all_to_all(crop_rows, 'tile', split_axis=1, concat_axis=0, tiled=True)  35.9 us
    all_to_all x3, local copies, waits for them, and re-layouts, per_device(): lax.all_to_all(crop_rows, 'tile', split_axis=1, concat_axis=0, tiled=True)  22.8 us
    ppermute x1, waiting for transfers between devices, from_behind(): return lax.ppermute(block, axis, route)  18.8 us
    all_gather x1, waiting for transfers between devices, per_device(): pre_grad = lax.all_gather(pre_own, 'tile', axis=1, tiled=True)  17.7 us
  transfers between devices with their start and end apart: 7, of which 5 were waited for; matrix products, arithmetic and copies ran while one was open for 45% of the time, Pallas kernels for 0%

commit v1 on v0

v1 whole, which is shorter than its diff:
```python
import functools

import jax
import jax.numpy as jnp
from jax import lax
from jax.experimental import pallas as pl
from jax.experimental.pallas import tpu as pltpu
from jax.sharding import PartitionSpec as P

WIN = 16
BINS = 7
ROWS_PAD = 56
GROUP = 16


def from_ahead(block, axis, distance):
    if distance == 0:
        return block
    size = lax.axis_size(axis)
    return lax.ppermute(block, axis, [(i, (i - distance) % size) for i in range(size)])


def halo_from_next(block, axis):
    size = lax.axis_size(axis)
    return lax.ppermute(block, axis, [(i + 1, i) for i in range(size - 1)])


def gelu_parts(hidden):
    factor = 0.7978845608028654
    cubic_term = 0.044715
    inner_term = factor * (hidden + cubic_term * hidden * hidden * hidden)
    tangent = jnp.tanh(inner_term)
    gelu_value = 0.5 * hidden * (1.0 + tangent)
    gelu_slope = 0.5 * (1.0 + tangent) + 0.5 * hidden * (1.0 - tangent * tangent) * factor * (
        1.0 + 3.0 * cubic_term * hidden * hidden
    )
    return (gelu_value, gelu_slope)


def crop_kernel(starts, width, cells_ref, geo_ref, maps_ref, out_ref, wide, stage):
    step = pl.program_id(0)

    @pl.when(step == 0)
    def _():
        def widen(r, carry):
            wide[r] = maps_ref[r].astype(jnp.float32)
            return carry

        lax.fori_loop(0, maps_ref.shape[0], widen, 0)

    shape = (ROWS_PAD, WIN * WIN)
    k = lax.broadcasted_iota(jnp.int32, shape, 0).astype(jnp.float32)
    i_bin = jnp.floor((k + 0.5) * (1.0 / BINS))
    j_bin = k - BINS * i_bin
    i_mid = i_bin + 0.5
    j_mid = j_bin + 0.5
    lane = lax.broadcasted_iota(jnp.int32, shape, 1)
    r_cell = (lane >> 4).astype(jnp.float32)
    q_cell = (lane & 15).astype(jnp.float32)
    for p in range(GROUP):
        n = step * GROUP + p
        row = cells_ref[0, n]
        col = cells_ref[1, n]
        row_w = jnp.maximum(0.0, 1.0 - jnp.abs(i_mid * geo_ref[1, n] + geo_ref[0, n] - r_cell))
        col_w = jnp.maximum(0.0, 1.0 - jnp.abs(j_mid * geo_ref[3, n] + geo_ref[2, n] - q_cell))
        weights = (row_w * col_w).astype(jnp.bfloat16)
        window = jnp.concatenate(
            [wide[row + r, pl.ds(col, WIN), :] for r in range(WIN)], axis=0
        ).astype(jnp.bfloat16)
        crop = jnp.dot(weights, window, preferred_element_type=jnp.float32)
        stage[pl.ds(p, ROWS_PAD, stride=GROUP), :] = crop
    for t, first in enumerate(starts):
        for m in range(width):
            at = (first + m) * GROUP
            out_ref[t, :, m * 128 : (m + 1) * 128] = stage[at : at + GROUP, :].astype(jnp.bfloat16)


def make_crops(cells, geo, maps, starts, width, capacity):
    tiles = len(starts)
    lanes = width * 128
    return pl.pallas_call(
        functools.partial(crop_kernel, starts, width),
        grid=(capacity // GROUP,),
        out_shape=jax.ShapeDtypeStruct((tiles, capacity, lanes), jnp.bfloat16),
        in_specs=[
            pl.BlockSpec(memory_space=pltpu.SMEM),
            pl.BlockSpec(memory_space=pltpu.SMEM),
            pl.BlockSpec(maps.shape, lambda g: (0, 0, 0)),
        ],
        out_specs=pl.BlockSpec((tiles, GROUP, lanes), lambda g: (0, g, 0)),
        scratch_shapes=[
            pltpu.VMEM(maps.shape, jnp.float32),
            pltpu.VMEM((ROWS_PAD * GROUP, 128), jnp.float32),
        ],
        compiler_params=pltpu.CompilerParams(
            dimension_semantics=("arbitrary",), vmem_limit_bytes=48 * 1024 * 1024
        ),
        cost_estimate=pl.CostEstimate(
            flops=capacity * ROWS_PAD * WIN * WIN * 128 * 16,
            bytes_accessed=2 * maps.size + 2 * tiles * capacity * lanes,
            transcendentals=0,
        ),
        name="crops",
    )(cells, geo, maps)


def per_device(
    proposal_boxes, level_plan, fine_map, coarse_map, first_weight, second_weight, upstream
):
    tile_count = lax.axis_size("tile")
    band = lax.axis_index("tile")
    num_props = level_plan.shape[1]
    capacity = max(num_props // 4, num_props // tile_count)
    fine_tile = fine_map[0]
    coarse = coarse_map[0]
    fine_rows, fine_cols, channels = fine_tile.shape
    coarse_rows, coarse_cols = (coarse.shape[0], coarse.shape[1])

    top_rows = jnp.concatenate([fine_tile[:WIN], coarse[:WIN]], axis=1)
    below_rows = halo_from_next(top_rows, "tile")

    share_feats = first_weight.shape[0]
    feats = share_feats * tile_count
    width = max(
        -(-((t + 1) * share_feats) // 128) - t * share_feats // 128 for t in range(tile_count)
    )
    starts = [min(t * share_feats // 128, feats // 128 - width) for t in range(tile_count)]
    lanes = width * 128
    feat_off = band * share_feats - 128 * jnp.minimum(
        band * share_feats // 128, feats // 128 - width
    )

    first_rows = lax.dynamic_update_slice(
        jnp.zeros((first_weight.shape[1], lanes), jnp.bfloat16),
        first_weight.T,
        (0, feat_off),
    )
    both = lax.all_gather(
        jnp.concatenate([first_rows, second_weight.T], axis=1), "dp", axis=0, tiled=True
    )
    first_all = both[:, :lanes]
    second_all = both[:, lanes:]

    fields = proposal_boxes[0]
    levels = level_plan[0]
    owner = fields[0] // (4 * fine_rows)
    members = (owner[:, None] == jnp.arange(tile_count, dtype=jnp.int32)[None, :]).astype(jnp.int32)
    rank = jnp.sum((jnp.cumsum(members, axis=0) - 1) * members, axis=1)
    relative = lax.rem(owner - band + tile_count, tile_count)
    slot_id = relative * capacity + rank
    slots = tile_count * capacity
    chosen = slot_id[None, :] == jnp.arange(slots, dtype=jnp.int32)[:, None]
    upstream_slots = jnp.dot(
        chosen.astype(jnp.bfloat16), upstream[0], preferred_element_type=jnp.float32
    ).astype(jnp.bfloat16)
    mine = chosen[:capacity].astype(jnp.int32)
    top, left, height, box_width = (
        jnp.sum(mine * fields[f][None, :], axis=1) for f in range(4)
    )
    level = jnp.sum(mine * levels[None, :], axis=1)

    stride = jnp.where(level == 0, 4, 8).astype(jnp.int32)
    is_fine = level == 0
    first_row = top // stride
    local_row = jnp.clip(
        first_row - band * jnp.where(is_fine, fine_rows, coarse_rows),
        0,
        jnp.where(is_fine, fine_rows, coarse_rows) - 1,
    )
    first_col = jnp.minimum(left // stride, jnp.where(is_fine, fine_cols, coarse_cols) - WIN)
    cells = jnp.stack(
        [local_row + jnp.where(is_fine, 0, fine_rows + WIN), first_col], axis=0
    ).astype(jnp.int32)
    stride_float = stride.astype(jnp.float32)
    geo = jnp.stack(
        [
            top.astype(jnp.float32) / stride_float - first_row.astype(jnp.float32),
            height.astype(jnp.float32) / (7.0 * stride_float),
            left.astype(jnp.float32) / stride_float - first_col.astype(jnp.float32),
            box_width.astype(jnp.float32) / (7.0 * stride_float),
        ],
        axis=0,
    )

    side = ((0, 0), (0, fine_cols - coarse_cols), (0, 0))
    maps = jnp.concatenate(
        [
            fine_tile,
            below_rows[:, :fine_cols],
            jnp.pad(coarse, side),
            jnp.pad(below_rows[:, fine_cols:], side),
        ],
        axis=0,
    )
    crop_blocks = make_crops(cells, geo, maps, starts, width, capacity)
    own_feats = jnp.concatenate(
        [
            from_ahead(
                lax.dynamic_index_in_dim(
                    crop_blocks, lax.rem(band - d + tile_count, tile_count), 0, keepdims=False
                ),
                "tile",
                d,
            )
            for d in range(tile_count)
        ],
        axis=0,
    )

    partial_hidden = lax.dot_general(
        own_feats, first_all, (((1,), (1,)), ((), ())), preferred_element_type=jnp.float32
    ).astype(jnp.bfloat16)
    share = second_weight.shape[0]

    def in_my_order(block, d):
        return jnp.roll(block, d * capacity, axis=0) if d else block

    hidden_own = 0.0
    for d in range(tile_count):
        to = lax.rem(band - d + tile_count, tile_count)
        piece = lax.dynamic_slice_in_dim(partial_hidden, to * share, share, axis=1)
        hidden_own = hidden_own + in_my_order(from_ahead(piece, "tile", d), d).astype(jnp.float32)
    gelu_value, gelu_slope = gelu_parts(hidden_own)
    activated = gelu_value.astype(jnp.bfloat16)
    back_grad = jnp.dot(upstream_slots, second_all, preferred_element_type=jnp.float32)
    pre_own = (back_grad * gelu_slope).astype(jnp.bfloat16)
    ahead = [in_my_order(from_ahead(pre_own, "tile", d), d) for d in range(tile_count)]
    twice = jnp.concatenate(ahead + ahead[:-1], axis=1)
    pre_grad = lax.dynamic_slice_in_dim(
        twice, lax.rem(tile_count - band, tile_count) * share, tile_count * share, axis=1
    )
    over_rows = (((0,), (0,)), ((), ()))
    second_part = lax.dot_general(
        upstream_slots, activated, over_rows, preferred_element_type=jnp.float32
    ).astype(jnp.bfloat16)
    first_part = lax.dot_general(
        pre_grad, own_feats, over_rows, preferred_element_type=jnp.float32
    ).astype(jnp.bfloat16)
    summed = lax.psum_scatter(
        jnp.concatenate([first_part, second_part], axis=1), "dp", scatter_dimension=0, tiled=True
    ).astype(jnp.float32)
    first_grad = lax.dynamic_slice_in_dim(summed[:, :lanes], feat_off, share_feats, axis=1).T
    second_grad = summed[:, lanes:].T
    return (first_grad, second_grad)


def solution(mesh):
    placed = (
        P("dp", None, None),
        P("dp", None),
        P("dp", "tile", None, None),
        P("dp", "tile", None, None),
        P("tile", "dp"),
        P("tile", "dp"),
        P("dp", None, None),
    )
    return jax.shard_map(
        per_device,
        mesh=mesh,
        in_specs=placed,
        out_specs=(P("tile", "dp"), P("tile", "dp")),
        check_vma=False,
    )
```

time: 591 us -> 264 us (0.45)
  matrix products: 213 us -> 24 us
  waiting for transfers between devices: 270 us -> 174 us
  local copies, waits for them, and re-layouts: 59.2 us -> 14.1 us
  blocking collectives: 15.2 us -> 0 us
  Pallas kernels: 0 us -> 13.2 us
  other arithmetic: 9.25 us -> 21.3 us
    dot_general x36 -> x5, matrix products: 213 us -> 24 us  [the longest x1 9.24 us: per_device(): lax.dot_general(pre_grad, own_feats, over_rows, preferred_element_type=jn...]
    ppermute x1 -> x4, waiting for transfers between devices: 18.8 us -> 80.9 us  [the longest x3 56.4 us: from_ahead(): lax.ppermute(block, axis, [(i, (i - distance) % size) for i in range(size)])]
    unnamed x6 -> x2, waiting for transfers between devices: 55.9 us -> 0.03 us
    reduce_scatter x1, waiting for transfers between devices: 142 us -> 93.4 us  [per_device(): lax.psum_scatter(jnp.concatenate([first_part, second_part], axis=1), 'dp'...]
    all_to_all x1 -> x0, waiting for transfers between devices: 35.9 us -> none  [per_device(): lax.all_to_all(crop_rows, 'tile', split_axis=1, concat_axis=0, tiled=True)]
    all_to_all x4 -> x0, local copies, waits for them, and re-layouts: 22.8 us -> none  [the longest x3 22.8 us: per_device(): lax.all_to_all(crop_rows, 'tile', split_axis=1, concat_axis=0, tiled=True)]
    all_gather x3 -> x1, waiting for transfers between devices: 17.8 us -> 0.01 us  [per_device(): lax.all_gather(jnp.concatenate([first_rows, second_weight.T], axis=1), 'd...]
    all_to_all x1 -> x0, blocking collectives: 15.2 us -> none  [per_device(): lax.all_to_all(partial_hidden.astype(jnp.bfloat16), 'tile', split_axis=1,...]
  transfers between devices with their start and end apart: 7 -> 6, of which waited for: 5 -> 5; matrix products, arithmetic and copies ran while one was open for 45% -> 8% of each run, Pallas kernels for 0% -> 5%
where the time goes in v1:
time: 264 us; the launch traced here: 263 us
  waiting for transfers between devices  174 us (66%)
  matrix products  24 us (9%)
  other arithmetic  21.3 us (8%)
  between operations  14.4 us (5%)
  local copies, waits for them, and re-layouts  14.1 us (5%)
  Pallas kernels  13.2 us (5%)
    reduce_scatter x1, waiting for transfers between devices, per_device(): lax.psum_scatter(jnp.concatenate([first_part, second_part], axis=1), 'dp'...  93.4 us
    ppermute x3, waiting for transfers between devices, from_ahead(): lax.ppermute(block, axis, [(i, (i - distance) % size) for i in range(size)])  56.4 us
    ppermute x1, waiting for transfers between devices, halo_from_next(): return lax.ppermute(block, axis, [(i + 1, i) for i in range(size - 1)])  24.5 us
    pallas_call x1, Pallas kernels, make_crops(): pl.pallas_call(functools.partial(crop_kernel, starts, width), grid=(capac...  13.2 us
    dot_general x1, matrix products, per_device(): lax.dot_general(pre_grad, own_feats, over_rows, preferred_element_type=jn...  9.24 us
    concatenate x1, other arithmetic, per_device(): jnp.concatenate([fine_tile, below_rows[:, :fine_cols], jnp.pad(coarse, si...  8.77 us
    dot_general x1, matrix products, per_device(): lax.dot_general(own_feats, first_all, (((1,), (1,)), ((), ())), preferred...  7.07 us
    concatenate x1, other arithmetic, per_device(): jnp.concatenate([first_part, second_part], axis=1)  6.72 us
  transfers between devices with their start and end apart: 6, of which 5 were waited for; matrix products, arithmetic and copies ran while one was open for 8% of the time, Pallas kernels for 5%

profile of v1, /device:TPU:0, one launch (start us, length us, event | category | flops | bytes accessed | tf_op | source)
XLA Modules:
  0.0 263.4 jit_solution(14502915766918753195)
XLA Ops:
  7.3 5.0 %dynamic_update_slice.3 = bf16[64,3200]{1,0:T(8,128)(2,1)S(1)} dynamic-update-slice(bf16[64,3200]{1,0:T(8,128)(2,1)S(1)} %broadcast_in_dim.33, bf16[64,3136]{1,0:T(8,128)(2,1)} %bitcast.56, s32[]{:T(128)} %constant.88.clone.1, s32[]{:T(128)S(6)} %select_n.146) | dynamic-update-slice | bytes 802820 | tf_op jit(solution)/shard_map/dynamic_update_slice | solution.py:133
  12.3 1.7 pad_maximum_fusion.8
  14.3 1.1 pad_maximum_fusion.6
  15.4 1.3 collective-permute-start
  16.7 0.6 reduce-window.6
  17.4 0.2 slice_reduce_fusion
  17.6 0.2 reduce-window.9
  18.1 0.4 select_reduce_fusion.1
  18.9 24.5 %collective-permute-done = bf16[16,252,128]{2,0,1:T(8,128)(2,1)} collective-permute-done((bf16[16,252,128]{2,0,1:T(8,128)(2,1)}, bf16[16,252,128]{2,0,1:T(8,128)(2,1)}, u32[]{:S(2)}, u32[]{:S(2)}) %collective-permute-start) | collective-permute-done | bytes 1032224 | tf_op jit(solution)/shard_map/ppermute | solution.py:25
  43.4 1.2 slice.94
  44.8 1.0 slice.95
  45.9 8.8 %fusion.6.maps_ref = bf16[95,168,128]{2,1,0:T(8,128)(2,1)} fusion(bf16[16,84,128]{2,1,0:T(8,128)(2,1)S(1)} %copy.30, bf16[21,84,128]{2,1,0:T(8,128)(2,1)} %bitcast.54, bf16[16,168,128]{2,1,0:T(8,128)(2,1)S(1)} %copy.29, bf16[42,168,128]{2,1,0:T(8,128)(2,1)S(1)} %bitcast.52), kind=kLoop, calls=%fused_computation.11 | loop fusion | flops 28600320 | bytes 7375872 | tf_op jit(solution)/shard_map/concatenate | solution.py:186
  54.7 13.2 %crops.1 = bf16[2,256,3200]{2,1,0:T(8,128)(2,1)S(1)} custom-call(s32[2,256]{1,0:T(2,128)S(1)} %pad_add_fusion.cells_ref, f32[4,256]{1,0:T(4,128)S(1)} %pad_maximum_fusion.10.geo_ref, bf16[95,168,128]{2,1,0:T(8,128)(2,1)} %fusion.6.maps_ref), custom_call_target="tpu_custom_call" | custom-call | flops 7516192768 | bytes 7362560 | tf_op jit(solution)/shard_map/crops/pallas_call | solution.py:81
  67.9 1.4 dynamic-slice_bitcast_fusion.1
  69.3 37.3 %collective-permute-done.1 = bf16[256,3200]{1,0:T(8,128)(2,1)} collective-permute-done((bf16[256,3200]{1,0:T(8,128)(2,1)}, bf16[256,3200]{1,0:T(8,128)(2,1)}, u32[]{:S(2)}, u32[]{:S(2)}) %collective-permute-start.1) | collective-permute-done | bytes 1638432 | tf_op jit(solution)/shard_map/ppermute | solution.py:20
  106.6 7.1 %fusion.7 = bf16[512,1024]{0,1:T(8,128)(2,1)S(1)} fusion(bf16[1024,3712]{1,0:T(8,128)(2,1)} %all-gather.2.cloned.1.call-done, bf16[256,3200]{1,0:T(8,128)(2,1)} %collective-permute-done.1, bf16[256,3200]{1,0:T(8,128)(2,1)S(1)} %get-tuple-element.11), kind=kOutput, calls=%fused_computation.23 | convolution fusion | flops 3362521088 | bytes 10878976 | tf_op jit(solution)/shard_map/dot_general | solution.py:210
  113.7 1.0 copy-done.2
  114.7 0.8 constant_dynamic-slice_fusion
  115.5 0.3 collective-permute-start.2
  115.8 0.7 convolution_convert_fusion.1
  116.5 11.4 %collective-permute-done.2 = bf16[512,512]{0,1:T(8,128)(2,1)S(1)} collective-permute-done((bf16[512,512]{0,1:T(8,128)(2,1)}, bf16[512,512]{0,1:T(8,128)(2,1)S(1)}, u32[]{:S(2)}, u32[]{:S(2)}) %collective-permute-start.2) | collective-permute-done | bytes 524320 | tf_op jit(solution)/shard_map/ppermute | solution.py:20
  128.0 3.6 %fusion.10 = bf16[512,512]{0,1:T(8,128)(2,1)} fusion(bf16[512,1024]{1,0:T(8,128)(2,1)S(1)} %convolution_convert_fusion.1, bf16[1024,3712]{1,0:T(8,128)(2,1)} %all-gather.2.cloned.1.call-done, bf16[512,1024]{0,1:T(8,128)(2,1)} %copy-done.2, s32[]{:T(128)S(6)} %select_n.156, bf16[256,512]{0,1:T(8,128)(2,1)S(1)} %get-tuple-element.16, ...), kind=kOutput, calls=%fused_computation.25 | convolution fusion | flops 543424512 | bytes 3670020 | tf_op jit(solution)/shard_map/dot_general | solution.py:225
  131.6 0.6 collective-permute-start.3
  132.2 3.3 %convolution_convert_fusion.2 = bf16[1024,512]{1,0:T(8,128)(2,1)} fusion(bf16[512,1024]{1,0:T(8,128)(2,1)} %copy-done.6, bf16[512,1024]{0,1:T(8,128)(2,1)} %copy-done.2, s32[]{:T(128)S(6)} %select_n.156, bf16[256,512]{0,1:T(8,128)(2,1)} %copy-done.3, bf16[256,512]{0,1:T(8,128)(2,1)S(1)} %get-tuple-element.15), kind=kOutput, calls=%fused_computation.22 | convolution fusion | flops 541327360 | bytes 3145732 | tf_op jit(solution)/shard_map/dot_general | solution.py:233
  135.5 7.7 %collective-permute-done.3 = bf16[512,512]{0,1:T(8,128)(2,1)S(1)} collective-permute-done((bf16[512,512]{0,1:T(8,128)(2,1)}, bf16[512,512]{0,1:T(8,128)(2,1)S(1)}, u32[]{:S(2)}, u32[]{:S(2)}) %collective-permute-start.3) | collective-permute-done | bytes 524320 | tf_op jit(solution)/shard_map/ppermute | solution.py:20
  143.2 9.2 %convolution_convert_fusion = bf16[1024,3200]{1,0:T(8,128)(2,1)} fusion(bf16[256,3200]{1,0:T(8,128)(2,1)} %collective-permute-done.1, bf16[256,3200]{1,0:T(8,128)(2,1)S(1)} %get-tuple-element.11, s32[]{:T(128)S(6)} %select_n.158, bf16[512,512]{0,1:T(8,128)(2,1)} %fusion.10, bf16[256,512]{0,1:T(8,128)(2,1)S(1)} %get-tuple-element.14, ...), kind=kOutput, calls=%fused_computation.7 | convolution fusion | flops 3369467904 | bytes 10878980 | tf_op jit(solution)/shard_map/dot_general | solution.py:236
  152.5 6.7 %pad_maximum_fusion = bf16[1024,3712]{1,0:T(8,128)(2,1)} fusion(bf16[1024,512]{1,0:T(8,128)(2,1)} %convolution_convert_fusion.2, bf16[1024,3200]{1,0:T(8,128)(2,1)} %convolution_convert_fusion), kind=kLoop, calls=%fused_computation.6 | loop fusion | flops 15204352 | bytes 15204352 | tf_op jit(solution)/shard_map/concatenate | solution.py:240
  159.2 93.4 %reduce-scatter.2.cloned.1.call-done = bf16[64,3712]{1,0:T(8,128)(2,1)} async-done(((bf16[1024,3712]{1,0:T(8,128)(2,1)}), bf16[64,3712]{1,0:T(8,128)(2,1)}) %reduce-scatter.2.cloned.1.call-update) | async-done | bytes 475152 | tf_op jit(solution)/shard_map/reduce_scatter | solution.py:239
  252.6 1.1 slice.101
  253.6 1.2 dynamic-slice_bitcast_fusion.2
  254.8 1.1 convert_element_type.147
  255.9 0.7 slice_bitcast_fusion
  (48 shorter events, 1.4 us)
Async XLA Ops:
  7.2 108.6 %copy-start = (bf16[1,512,1024]{2,1,0:T(8,128)(2,1)S(1)}, bf16[1,512,1024]{2,1,0:T(8,128)(2,1)}, u32[]{:S(2)}) copy-start(bf16[1,512,1024]{2,1,0:T(8,128)(2,1)} %param.13) | copy-start | bytes 3145732
  7.2 6.9 %slice-start = ((bf16[1,42,168,128]{3,2,1,0:T(8,128)(2,1)}), bf16[1,16,168,128]{3,2,1,0:T(8,128)(2,1)S(1)}, s32[]{:S(2)}) async-start(bf16[1,42,168,128]{3,2,1,0:T(8,128)(2,1)} %param.9), calls=%async_computation.3 | async-start | bytes 1376256 | tf_op jit(solution)/shard_map/slice | solution.py:119
  7.2 7.0 %slice-start.1 = ((bf16[1,21,84,128]{3,2,1,0:T(8,128)(2,1)}), bf16[1,16,84,128]{3,2,1,0:T(8,128)(2,1)S(1)}, s32[]{:S(2)}) async-start(bf16[1,21,84,128]{3,2,1,0:T(8,128)(2,1)} %param.10), calls=%async_computation.4 | async-start | bytes 720896 | tf_op jit(solution)/shard_map/slice | solution.py:119
  7.2 99.4 %all-gather.2.cloned.1.call-start = ((), (), s32[]{:S(2)}) async-start(), calls=%async_computation.1 | async-start | bytes 8077312 | tf_op jit(solution)/shard_map/all_gather | solution.py:138
  7.3 9.3 %copy-start.4 = (s32[1,4,512]{2,1,0:T(4,128)S(1)}, s32[1,4,512]{2,1,0:T(4,128)}, u32[]{:S(2)}) copy-start(s32[1,4,512]{2,1,0:T(4,128)} %param.7) | copy-start | bytes 24580
  12.3 5.8 %copy-start.5 = (s32[1,512]{1,0:T(1,128)S(1)}, s32[1,512]{1,0:T(1,128)}, u32[]{:S(2)}) copy-start(s32[1,512]{1,0:T(1,128)} %param.8) | copy-start | bytes 6148
  14.0 238.6 %reduce-scatter.2.cloned.1.call-start = ((), (), s32[]{:S(2)}) async-start(), calls=%async_computation.2 | async-start | bytes 8077312 | tf_op jit(solution)/shard_map/reduce_scatter | solution.py:239
  14.2 31.7 %copy-start.1 = (bf16[1,42,168,128]{3,2,1,0:T(8,128)(2,1)S(1)}, bf16[1,42,168,128]{3,2,1,0:T(8,128)(2,1)}, u32[]{:S(2)}) copy-start(bf16[1,42,168,128]{3,2,1,0:T(8,128)(2,1)} %param.9) | copy-start | bytes 5419012
  15.4 28.0 %collective-permute-start = (bf16[16,252,128]{2,0,1:T(8,128)(2,1)}, bf16[16,252,128]{2,0,1:T(8,128)(2,1)}, u32[]{:S(2)}, u32[]{:S(2)}) collective-permute-start(bf16[16,252,128]{2,0,1:T(8,128)(2,1)} %pad_maximum_fusion.6), channel_id=1, source_target_pairs={{1,0},{3,2},{5,4},{7,6},{9,8},{11,10},{13,12},{15,14},{17,16},{19,... | collective-permute-start | bytes 3096584 | tf_op jit(solution)/shard_map/ppermute | solution.py:25
  69.3 37.3 %collective-permute-start.1 = (bf16[256,3200]{1,0:T(8,128)(2,1)}, bf16[256,3200]{1,0:T(8,128)(2,1)}, u32[]{:S(2)}, u32[]{:S(2)}) collective-permute-start(bf16[256,3200]{1,0:T(8,128)(2,1)} %get-tuple-element.12), channel_id=1, source_target_pairs={{0,1},{1,0},{2,3},{3,2},{4,5},{5,4},{6,7},{7,6},{8,9},{9,8},{10,11... | collective-permute-start | bytes 4915208 | tf_op jit(solution)/shard_map/ppermute | solution.py:20
  113.7 1.0 copy-start.2
  115.5 12.5 %collective-permute-start.2 = (bf16[512,512]{0,1:T(8,128)(2,1)}, bf16[512,512]{0,1:T(8,128)(2,1)S(1)}, u32[]{:S(2)}, u32[]{:S(2)}) collective-permute-start(bf16[512,512]{0,1:T(8,128)(2,1)} %constant_dynamic-slice_fusion), channel_id=1, source_target_pairs={{0,1},{1,0},{2,3},{3,2},{4,5},{5,4},{6,7},{7,6},{8,9},{9,8},{10,11... | collective-permute-start | bytes 1572872 | tf_op jit(solution)/shard_map/ppermute | solution.py:20
  116.5 15.1 %copy-start.6 = (bf16[512,1024]{1,0:T(8,128)(2,1)}, bf16[512,1024]{1,0:T(8,128)(2,1)S(1)}, u32[]{:S(2)}) copy-start(bf16[512,1024]{1,0:T(8,128)(2,1)S(1)} %convolution_convert_fusion.1) | copy-start | bytes 3145732
  128.0 3.6 %copy-start.3 = (bf16[256,512]{0,1:T(8,128)(2,1)}, bf16[256,512]{0,1:T(8,128)(2,1)S(1)}, u32[]{:S(2)}) copy-start(bf16[256,512]{0,1:T(8,128)(2,1)S(1)} %get-tuple-element.16) | copy-start | bytes 786436
  131.6 11.6 %collective-permute-start.3 = (bf16[512,512]{0,1:T(8,128)(2,1)}, bf16[512,512]{0,1:T(8,128)(2,1)S(1)}, u32[]{:S(2)}, u32[]{:S(2)}) collective-permute-start(bf16[512,512]{0,1:T(8,128)(2,1)} %fusion.10), channel_id=1, source_target_pairs={{0,1},{1,0},{2,3},{3,2},{4,5},{5,4},{6,7},{7,6},{8,9},{9,8},{10,11... | collective-permute-start | bytes 1572872 | tf_op jit(solution)/shard_map/ppermute | solution.py:20
Sparse Core Ops, SparseCore 0:
  14.1 72.6 all-gather.1
  159.3 93.2 reduce-scatter.1
